TPU v7x, 128 devices: a whole 4x4x4 slice. The times are simulated.
128 devices in a mesh: walk: 16 (over y_hi, z, core), band: 8 (over y_lo, x).
Axes of the slice: x: 4, y: 4 (y_hi: 2, y_lo: 2; y = y_hi * 2 + y_lo), z: 4, core: 2. Of those that a mesh axis runs over, the one named last changes fastest.
Arguments:
- positions: float32 [2, 49152], P(None, 'walk'), may hold values from 0 to 1
- coefficients: bfloat16 [2, 18432, 1024], P(None, 'walk', 'band')
- lattice: int32 [2, 18432], replicated, may hold values from -76 to 76
- spin_labels: int32 [49152], P('walk'), may hold values from 0 to 1
- occupied: int32 [2, 48], replicated, may hold values from 0 to 1023
- features: bfloat16 [49152, 256], P('walk'), may hold values from -6 to 6
- orbital_head: bfloat16 [256, 192], replicated, may hold values from -0.029907227 to 0.029907227
Outputs:
- gradient: float32 [256, 192], replicated
All inputs are finite; a program needn't handle non-finite values.
Results may differ from a plain program's by a relative error of at most 0.0003.
Values may be sent and summed in bfloat16 or wider, within the bound.
No kernel may reach another device: no remote copies, remote signals or barrier semaphores. Data moves between devices by JAX's collectives and lax.ppermute only.
A program may use at most 128 MiB of HBM per device.

v0:
```python
import jax
import jax.numpy as jnp
from jax import lax
from jax.sharding import PartitionSpec as P

E = 96
TWO_PI = 6.283185307179586


def orbital_block(pos_x, pos_y, lat_x, lat_y, right_cos, right_sin):
    phase_angle = TWO_PI * (pos_x[:, None] * lat_x[None, :] + pos_y[:, None] * lat_y[None, :])
    cosine = jnp.cos(phase_angle)
    sine_part = jnp.sin(phase_angle)
    first = jnp.dot(
        cosine, right_cos, precision=lax.Precision.HIGHEST, preferred_element_type=jnp.float32
    )
    second = jnp.dot(
        sine_part, right_sin, precision=lax.Precision.HIGHEST, preferred_element_type=jnp.float32
    )
    return first + second


def spin_columns(orbitals, spin_labels):
    orbital_count = orbitals.shape[1] // 4
    spin_up = (spin_labels == 0)[:, None]
    real_pick = jnp.where(
        spin_up, orbitals[:, :orbital_count], orbitals[:, orbital_count : 2 * orbital_count]
    )
    imag_pick = jnp.where(
        spin_up,
        orbitals[:, 2 * orbital_count : 3 * orbital_count],
        orbitals[:, 3 * orbital_count :],
    )
    return jnp.concatenate([real_pick, imag_pick], axis=1)


def fit_from_target(target, spin_labels, features, orbital_head, walkers):
    half_width = target.shape[1]
    spin_up = (spin_labels == 0)[:, None]
    net_all = jnp.dot(features, orbital_head, preferred_element_type=jnp.float32)
    net_value = jnp.where(spin_up, net_all[:, :half_width], net_all[:, half_width:])
    scaled = (net_value - target) / walkers
    blank_rows = jnp.zeros_like(scaled)
    spread_rows = jnp.concatenate(
        [jnp.where(spin_up, scaled, blank_rows), jnp.where(spin_up, blank_rows, scaled)], axis=1
    )
    return lax.dot_general(
        features.astype(jnp.float32),
        spread_rows,
        (((0,), (0,)), ((), ())),
        precision=lax.Precision.HIGHEST,
        preferred_element_type=jnp.float32,
    )


def fit_gradient(orbitals, spin_labels, features, orbital_head, walkers):
    target = spin_columns(orbitals, spin_labels)
    return fit_from_target(target, spin_labels, features, orbital_head, walkers)


def local(positions, coefficients, lattice, spin_labels, occupied, features, orbital_head):
    walk_count = lax.axis_size("walk")
    band_count = lax.axis_size("band")
    band_index = lax.axis_index("band")
    occ_flat = occupied.reshape(-1)
    wave_count = lattice.shape[1]
    gathered = lax.all_gather(coefficients, "walk", axis=1, tiled=True)
    band_panel = lax.all_to_all(gathered, "band", split_axis=1, concat_axis=2, tiled=True)
    picked = jnp.take(band_panel, occ_flat, axis=2)
    local_lattice = lax.dynamic_slice_in_dim(
        lattice, band_index * (wave_count // band_count), wave_count // band_count, 1
    )
    right_cos = jnp.concatenate([picked[0], picked[1]], axis=1).astype(jnp.float32)
    right_sin = jnp.concatenate([-picked[1], picked[0]], axis=1).astype(jnp.float32)
    lat_x = local_lattice[0].astype(jnp.float32)
    lat_y = local_lattice[1].astype(jnp.float32)
    local_count = positions.shape[1]
    block_rows = min(384, local_count)
    block_count = local_count // block_rows
    pos_x = positions[0].reshape(block_count, block_rows)
    pos_y = positions[1].reshape(block_count, block_rows)
    partial_value = lax.map(
        lambda coords: orbital_block(coords[0], coords[1], lat_x, lat_y, right_cos, right_sin),
        (pos_x, pos_y),
    )
    partial_value = partial_value.reshape(local_count, right_cos.shape[1])
    walkers = float(walk_count * local_count // E)
    orbitals = lax.psum(partial_value, "band")
    gradient = fit_gradient(orbitals, spin_labels, features, orbital_head, walkers)
    return lax.psum(gradient, "walk")


def solution(mesh):
    return jax.shard_map(
        local,
        mesh=mesh,
        in_specs=(
            P(None, "walk"),
            P(None, "walk", "band"),
            P(),
            P("walk"),
            P(),
            P("walk", None),
            P(),
        ),
        out_specs=P(),
        check_vma=False,
    )
```

profile of v0, /device:TPU:0, one launch (start us, length us, event | category | flops | bytes accessed | tf_op | source)
XLA Modules:
  0.0 891.4 jit_solution(2126646476932792642)
XLA Ops:
  12.7 79.9 %all-gather.2.cloned.1.call-done = bf16[2,18432,128]{2,0,1:T(2,128)(2,1)} async-done(((bf16[2,1152,128]{2,0,1:T(2,128)(2,1)}), bf16[2,18432,128]{2,0,1:T(2,128)(2,1)}) %all-gather.2.cloned.1.call-update) | async-done | bytes 9437200 | tf_op jit(solution)/shard_map/all_gather | solution.py:67
  98.9 105.0 %all-to-all-done = bf16[2,18432,128]{2,0,1:T(2,128)(2,1)} async-done(((bf16[2,18432,128]{2,0,1:T(2,128)(2,1)}), bf16[2,18432,128]{2,0,1:T(2,128)(2,1)}, u32[]{:S(2)}, u32[]{:S(2)}) %all-to-all-start) | async-done | bytes 9437216 | tf_op jit(solution)/shard_map/all_to_all | solution.py:68
  203.9 10.1 %copy.32 = bf16[2,18432,128]{2,1,0:T(8,128)(2,1)} copy(bf16[2,18432,128]{2,0,1:T(2,128)(2,1)} %all-to-all-done) | data formatting | bytes 18874368 | tf_op jit(solution)/shard_map/all_to_all | solution.py:68
  214.0 12.9 %copy.33 = bf16[2,2304,8,128]{1,3,2,0:T(8,128)(2,1)} copy(bf16[2,2304,8,128]{3,1,2,0:T(8,128)(2,1)} %bitcast.33) | data formatting | bytes 18874368 | tf_op jit(solution)/shard_map/all_to_all | solution.py:68
  226.9 18.4 %copy.34 = bf16[2,2304,1024]{1,0,2:T(2,128)(2,1)} copy(bf16[2,2304,1024]{1,2,0:T(8,128)(2,1)} %bitcast.34) | data formatting | bytes 18874368 | tf_op jit(solution)/shard_map/all_to_all | solution.py:68
  259.9 364.3 %while.10 = (s32[]{:T(128)}, f32[8,384,192]{1,0,2:T(8,128)}, f32[8,384]{1,0:T(8,128)S(1)}, f32[2304]{0:T(1024)S(1)}, f32[8,384]{1,0:T(8,128)S(1)}, /*index=5*/f3...) while((s32[]{:T(128)}, f32[8,384,192]{1,0,2:T(8,128)}, ...), condition=%wide.region_1.2_spmd, body=%wide.region_0.1_spmd.sunk | while | flops 4084015104 | bytes 12730505 | solution.py:82
  282.6 18.3 %fusion.54 = f32[384,192]{0,1:T(8,128)S(1)} fusion(f32[2304,192]{1,0:T(8,128)} %get-tuple-element.200, f32[2304]{0:T(1024)S(1)} %get-tuple-element.198, f32[384]{0:T(512)S(1)} %get-tuple-element.171, f32[2304]{0:T(1024)S(1)} %get-tuple-element.196, f32[384]{0:T(512)S(1)} %get-tuple-element.172), kind=kOutput, calls=%fused_computation.1.clone.1 | convolution fusion | flops 2041970688 | bytes 2085888 | tf_op jit(solution)/shard_map/while/body/eval_jaxpr/dot_general | solution.py:17
  300.9 16.4 %fusion.55 = f32[1,384,192]{1,2,0:T(8,128)S(1)} fusion(f32[384,192]{0,1:T(8,128)S(1)} %fusion.54, f32[2304,192]{1,0:T(8,128)S(1)} %copy-done.2, f32[2304]{0:T(1024)S(1)} %get-tuple-element.198, f32[384]{0:T(512)S(1)} %get-tuple-element.171, f32[2304]{0:T(1024)S(1)} %get-tuple-element.196, f32[384]{0:T(512)S(1)} %get-tuple-element.172), kind=kOutput, calls=%fused_computation.17.clone.1 | convolution fusion | flops 2042044416 | bytes 2380800 | tf_op jit(solution)/shard_map/while/body/eval_jaxpr/dot_general | solution.py:14
  317.7 7.3 dynamic_update_slice.5
  325.0 18.3 %fusion.54 = f32[384,192]{0,1:T(8,128)S(1)} fusion(f32[2304,192]{1,0:T(8,128)} %get-tuple-element.200, f32[2304]{0:T(1024)S(1)} %get-tuple-element.198, f32[384]{0:T(512)S(1)} %get-tuple-element.171, f32[2304]{0:T(1024)S(1)} %get-tuple-element.196, f32[384]{0:T(512)S(1)} %get-tuple-element.172), kind=kOutput, calls=%fused_computation.1.clone.1 | convolution fusion | flops 2041970688 | bytes 2085888 | tf_op jit(solution)/shard_map/while/body/eval_jaxpr/dot_general | solution.py:17
  343.3 16.4 %fusion.55 = f32[1,384,192]{1,2,0:T(8,128)S(1)} fusion(f32[384,192]{0,1:T(8,128)S(1)} %fusion.54, f32[2304,192]{1,0:T(8,128)S(1)} %copy-done.2, f32[2304]{0:T(1024)S(1)} %get-tuple-element.198, f32[384]{0:T(512)S(1)} %get-tuple-element.171, f32[2304]{0:T(1024)S(1)} %get-tuple-element.196, f32[384]{0:T(512)S(1)} %get-tuple-element.172), kind=kOutput, calls=%fused_computation.17.clone.1 | convolution fusion | flops 2042044416 | bytes 2380800 | tf_op jit(solution)/shard_map/while/body/eval_jaxpr/dot_general | solution.py:14
  360.0 7.3 dynamic_update_slice.5
  367.4 18.3 %fusion.54 = f32[384,192]{0,1:T(8,128)S(1)} fusion(f32[2304,192]{1,0:T(8,128)} %get-tuple-element.200, f32[2304]{0:T(1024)S(1)} %get-tuple-element.198, f32[384]{0:T(512)S(1)} %get-tuple-element.171, f32[2304]{0:T(1024)S(1)} %get-tuple-element.196, f32[384]{0:T(512)S(1)} %get-tuple-element.172), kind=kOutput, calls=%fused_computation.1.clone.1 | convolution fusion | flops 2041970688 | bytes 2085888 | tf_op jit(solution)/shard_map/while/body/eval_jaxpr/dot_general | solution.py:17
  385.7 16.4 %fusion.55 = f32[1,384,192]{1,2,0:T(8,128)S(1)} fusion(f32[384,192]{0,1:T(8,128)S(1)} %fusion.54, f32[2304,192]{1,0:T(8,128)S(1)} %copy-done.2, f32[2304]{0:T(1024)S(1)} %get-tuple-element.198, f32[384]{0:T(512)S(1)} %get-tuple-element.171, f32[2304]{0:T(1024)S(1)} %get-tuple-element.196, f32[384]{0:T(512)S(1)} %get-tuple-element.172), kind=kOutput, calls=%fused_computation.17.clone.1 | convolution fusion | flops 2042044416 | bytes 2380800 | tf_op jit(solution)/shard_map/while/body/eval_jaxpr/dot_general | solution.py:14
  402.4 7.3 dynamic_update_slice.5
  409.7 18.3 %fusion.54 = f32[384,192]{0,1:T(8,128)S(1)} fusion(f32[2304,192]{1,0:T(8,128)} %get-tuple-element.200, f32[2304]{0:T(1024)S(1)} %get-tuple-element.198, f32[384]{0:T(512)S(1)} %get-tuple-element.171, f32[2304]{0:T(1024)S(1)} %get-tuple-element.196, f32[384]{0:T(512)S(1)} %get-tuple-element.172), kind=kOutput, calls=%fused_computation.1.clone.1 | convolution fusion | flops 2041970688 | bytes 2085888 | tf_op jit(solution)/shard_map/while/body/eval_jaxpr/dot_general | solution.py:17
  428.1 16.4 %fusion.55 = f32[1,384,192]{1,2,0:T(8,128)S(1)} fusion(f32[384,192]{0,1:T(8,128)S(1)} %fusion.54, f32[2304,192]{1,0:T(8,128)S(1)} %copy-done.2, f32[2304]{0:T(1024)S(1)} %get-tuple-element.198, f32[384]{0:T(512)S(1)} %get-tuple-element.171, f32[2304]{0:T(1024)S(1)} %get-tuple-element.196, f32[384]{0:T(512)S(1)} %get-tuple-element.172), kind=kOutput, calls=%fused_computation.17.clone.1 | convolution fusion | flops 2042044416 | bytes 2380800 | tf_op jit(solution)/shard_map/while/body/eval_jaxpr/dot_general | solution.py:14
  444.8 7.3 dynamic_update_slice.5
  452.1 18.3 %fusion.54 = f32[384,192]{0,1:T(8,128)S(1)} fusion(f32[2304,192]{1,0:T(8,128)} %get-tuple-element.200, f32[2304]{0:T(1024)S(1)} %get-tuple-element.198, f32[384]{0:T(512)S(1)} %get-tuple-element.171, f32[2304]{0:T(1024)S(1)} %get-tuple-element.196, f32[384]{0:T(512)S(1)} %get-tuple-element.172), kind=kOutput, calls=%fused_computation.1.clone.1 | convolution fusion | flops 2041970688 | bytes 2085888 | tf_op jit(solution)/shard_map/while/body/eval_jaxpr/dot_general | solution.py:17
  470.4 16.4 %fusion.55 = f32[1,384,192]{1,2,0:T(8,128)S(1)} fusion(f32[384,192]{0,1:T(8,128)S(1)} %fusion.54, f32[2304,192]{1,0:T(8,128)S(1)} %copy-done.2, f32[2304]{0:T(1024)S(1)} %get-tuple-element.198, f32[384]{0:T(512)S(1)} %get-tuple-element.171, f32[2304]{0:T(1024)S(1)} %get-tuple-element.196, f32[384]{0:T(512)S(1)} %get-tuple-element.172), kind=kOutput, calls=%fused_computation.17.clone.1 | convolution fusion | flops 2042044416 | bytes 2380800 | tf_op jit(solution)/shard_map/while/body/eval_jaxpr/dot_general | solution.py:14
  487.2 7.3 dynamic_update_slice.5
  494.5 18.3 %fusion.54 = f32[384,192]{0,1:T(8,128)S(1)} fusion(f32[2304,192]{1,0:T(8,128)} %get-tuple-element.200, f32[2304]{0:T(1024)S(1)} %get-tuple-element.198, f32[384]{0:T(512)S(1)} %get-tuple-element.171, f32[2304]{0:T(1024)S(1)} %get-tuple-element.196, f32[384]{0:T(512)S(1)} %get-tuple-element.172), kind=kOutput, calls=%fused_computation.1.clone.1 | convolution fusion | flops 2041970688 | bytes 2085888 | tf_op jit(solution)/shard_map/while/body/eval_jaxpr/dot_general | solution.py:17
  512.8 16.4 %fusion.55 = f32[1,384,192]{1,2,0:T(8,128)S(1)} fusion(f32[384,192]{0,1:T(8,128)S(1)} %fusion.54, f32[2304,192]{1,0:T(8,128)S(1)} %copy-done.2, f32[2304]{0:T(1024)S(1)} %get-tuple-element.198, f32[384]{0:T(512)S(1)} %get-tuple-element.171, f32[2304]{0:T(1024)S(1)} %get-tuple-element.196, f32[384]{0:T(512)S(1)} %get-tuple-element.172), kind=kOutput, calls=%fused_computation.17.clone.1 | convolution fusion | flops 2042044416 | bytes 2380800 | tf_op jit(solution)/shard_map/while/body/eval_jaxpr/dot_general | solution.py:14
  529.5 7.3 dynamic_update_slice.5
  536.9 18.3 %fusion.54 = f32[384,192]{0,1:T(8,128)S(1)} fusion(f32[2304,192]{1,0:T(8,128)} %get-tuple-element.200, f32[2304]{0:T(1024)S(1)} %get-tuple-element.198, f32[384]{0:T(512)S(1)} %get-tuple-element.171, f32[2304]{0:T(1024)S(1)} %get-tuple-element.196, f32[384]{0:T(512)S(1)} %get-tuple-element.172), kind=kOutput, calls=%fused_computation.1.clone.1 | convolution fusion | flops 2041970688 | bytes 2085888 | tf_op jit(solution)/shard_map/while/body/eval_jaxpr/dot_general | solution.py:17
  555.2 16.4 %fusion.55 = f32[1,384,192]{1,2,0:T(8,128)S(1)} fusion(f32[384,192]{0,1:T(8,128)S(1)} %fusion.54, f32[2304,192]{1,0:T(8,128)S(1)} %copy-done.2, f32[2304]{0:T(1024)S(1)} %get-tuple-element.198, f32[384]{0:T(512)S(1)} %get-tuple-element.171, f32[2304]{0:T(1024)S(1)} %get-tuple-element.196, f32[384]{0:T(512)S(1)} %get-tuple-element.172), kind=kOutput, calls=%fused_computation.17.clone.1 | convolution fusion | flops 2042044416 | bytes 2380800 | tf_op jit(solution)/shard_map/while/body/eval_jaxpr/dot_general | solution.py:14
  571.9 7.3 dynamic_update_slice.5
  579.2 18.3 %fusion.54 = f32[384,192]{0,1:T(8,128)S(1)} fusion(f32[2304,192]{1,0:T(8,128)} %get-tuple-element.200, f32[2304]{0:T(1024)S(1)} %get-tuple-element.198, f32[384]{0:T(512)S(1)} %get-tuple-element.171, f32[2304]{0:T(1024)S(1)} %get-tuple-element.196, f32[384]{0:T(512)S(1)} %get-tuple-element.172), kind=kOutput, calls=%fused_computation.1.clone.1 | convolution fusion | flops 2041970688 | bytes 2085888 | tf_op jit(solution)/shard_map/while/body/eval_jaxpr/dot_general | solution.py:17
  597.6 16.4 %fusion.55 = f32[1,384,192]{1,2,0:T(8,128)S(1)} fusion(f32[384,192]{0,1:T(8,128)S(1)} %fusion.54, f32[2304,192]{1,0:T(8,128)S(1)} %copy-done.2, f32[2304]{0:T(1024)S(1)} %get-tuple-element.198, f32[384]{0:T(512)S(1)} %get-tuple-element.171, f32[2304]{0:T(1024)S(1)} %get-tuple-element.196, f32[384]{0:T(512)S(1)} %get-tuple-element.172), kind=kOutput, calls=%fused_computation.17.clone.1 | convolution fusion | flops 2042044416 | bytes 2380800 | tf_op jit(solution)/shard_map/while/body/eval_jaxpr/dot_general | solution.py:14
  614.3 7.3 dynamic_update_slice.5
  630.7 114.0 %all-reduce.3.cloned.1.call-done = f32[3072,192]{0,1:T(8,128)} async-done(((f32[3072,192]{0,1:T(8,128)}), f32[3072,192]{0,1:T(8,128)}) %all-reduce.3.cloned.1.call-update) | async-done | bytes 2359312 | tf_op jit(solution)/shard_map/psum | solution.py:88
  749.4 133.6 %all-reduce.5.cloned.1.call-done = f32[256,192]{0,1:T(8,128)} async-done(((f32[256,192]{0,1:T(8,128)}), f32[256,192]{0,1:T(8,128)}) %all-reduce.5.cloned.1.call-update) | async-done | bytes 196624 | tf_op jit(solution)/shard_map/psum | solution.py:90
  (77 shorter events, 42.4 us)
Async XLA Ops:
  6.5 621.9 %copy-start = (bf16[3072,256]{1,0:T(8,128)(2,1)S(1)}, bf16[3072,256]{1,0:T(8,128)(2,1)}, u32[]{:S(2)}) copy-start(bf16[3072,256]{1,0:T(8,128)(2,1)} %param.14) | copy-start | bytes 4718596
  6.5 86.0 %all-gather.2.cloned.1.call-start = ((), (), s32[]{:S(2)}) async-start(), calls=%async_computation.1 | async-start | bytes 10027008 | tf_op jit(solution)/shard_map/all_gather | solution.py:67
  12.6 85.0 %copy-start.6 = (s32[2,48]{1,0:T(2,128)S(1)}, s32[2,48]{1,0:T(2,128)}, u32[]{:S(2)}) copy-start(s32[2,48]{1,0:T(2,128)} %param.13) | copy-start | bytes 1156
  12.6 85.2 %copy-start.4 = (f32[2,3072]{1,0:T(2,128)S(1)}, f32[2,3072]{1,0:T(2,128)}, u32[]{:S(2)}) copy-start(f32[2,3072]{1,0:T(2,128)} %param.9) | copy-start | bytes 73732
  92.5 111.3 %all-to-all-start = ((bf16[2,18432,128]{2,0,1:T(2,128)(2,1)}), bf16[2,18432,128]{2,0,1:T(2,128)(2,1)}, u32[]{:S(2)}, u32[]{:S(2)}) async-start(bf16[2,18432,128]{2,0,1:T(2,128)(2,1)} %all-gather.2.cloned.1.call-done), calls=%async_computation | async-start | bytes 18874368 | tf_op jit(solution)/shard_map/all_to_all | solution.py:68
  97.6 647.1 %all-reduce.3.cloned.1.call-start = ((), (), s32[]{:S(2)}) async-start(), calls=%async_computation.2 | async-start | bytes 4718592 | tf_op jit(solution)/shard_map/psum | solution.py:88
  282.6 18.3 %copy-start.2 = (f32[2304,192]{1,0:T(8,128)S(1)}, f32[2304,192]{1,0:T(8,128)}, u32[]{:S(2)}) copy-start(f32[2304,192]{1,0:T(8,128)} %get-tuple-element.199) | copy-start | bytes 5308420 | tf_op jit(solution)/shard_map/while
  325.0 18.3 %copy-start.2 = (f32[2304,192]{1,0:T(8,128)S(1)}, f32[2304,192]{1,0:T(8,128)}, u32[]{:S(2)}) copy-start(f32[2304,192]{1,0:T(8,128)} %get-tuple-element.199) | copy-start | bytes 5308420 | tf_op jit(solution)/shard_map/while
  367.3 18.3 %copy-start.2 = (f32[2304,192]{1,0:T(8,128)S(1)}, f32[2304,192]{1,0:T(8,128)}, u32[]{:S(2)}) copy-start(f32[2304,192]{1,0:T(8,128)} %get-tuple-element.199) | copy-start | bytes 5308420 | tf_op jit(solution)/shard_map/while
  409.7 18.3 %copy-start.2 = (f32[2304,192]{1,0:T(8,128)S(1)}, f32[2304,192]{1,0:T(8,128)}, u32[]{:S(2)}) copy-start(f32[2304,192]{1,0:T(8,128)} %get-tuple-element.199) | copy-start | bytes 5308420 | tf_op jit(solution)/shard_map/while
  452.1 18.3 %copy-start.2 = (f32[2304,192]{1,0:T(8,128)S(1)}, f32[2304,192]{1,0:T(8,128)}, u32[]{:S(2)}) copy-start(f32[2304,192]{1,0:T(8,128)} %get-tuple-element.199) | copy-start | bytes 5308420 | tf_op jit(solution)/shard_map/while
  494.5 18.3 %copy-start.2 = (f32[2304,192]{1,0:T(8,128)S(1)}, f32[2304,192]{1,0:T(8,128)}, u32[]{:S(2)}) copy-start(f32[2304,192]{1,0:T(8,128)} %get-tuple-element.199) | copy-start | bytes 5308420 | tf_op jit(solution)/shard_map/while
  536.8 18.3 %copy-start.2 = (f32[2304,192]{1,0:T(8,128)S(1)}, f32[2304,192]{1,0:T(8,128)}, u32[]{:S(2)}) copy-start(f32[2304,192]{1,0:T(8,128)} %get-tuple-element.199) | copy-start | bytes 5308420 | tf_op jit(solution)/shard_map/while
  579.2 18.3 %copy-start.2 = (f32[2304,192]{1,0:T(8,128)S(1)}, f32[2304,192]{1,0:T(8,128)}, u32[]{:S(2)}) copy-start(f32[2304,192]{1,0:T(8,128)} %get-tuple-element.199) | copy-start | bytes 5308420 | tf_op jit(solution)/shard_map/while
  627.7 0.7 copy-start.5
  627.7 0.9 copy-start.3
  627.8 255.3 %all-reduce.5.cloned.1.call-start = ((), (), s32[]{:S(2)}) async-start(), calls=%async_computation.3 | async-start | bytes 393216 | tf_op jit(solution)/shard_map/psum | solution.py:90
  744.7 2.4 copy-start.1
Sparse Core Ops, SparseCore 0:
  12.7 79.7 all-gather.1
  627.9 116.7 all-reduce.2
  749.6 133.4 all-reduce.4
where the time goes:
time: 901 us; the launch traced here: 891 us
  waiting for transfers between devices  433 us (48%)
  matrix products  282 us (31%)
  local copies, waits for them, and re-layouts  127 us (14%)
  loops' own time  25.6 us (3%)
  between operations  13.4 us (1%)
    dot_general x8, matrix products, orbital_block(): jnp.dot(sine_part, right_sin, precision=lax.Precision.HIGHEST, preferred_...  146 us
    psum x1, waiting for transfers between devices, local(): return lax.psum(gradient, 'walk')  134 us
    dot_general x8, matrix products, orbital_block(): jnp.dot(cosine, right_cos, precision=lax.Precision.HIGHEST, preferred_ele...  131 us
    psum x1, waiting for transfers between devices, local(): orbitals = lax.psum(partial_value, 'band')  114 us
    all_to_all x1, waiting for transfers between devices, local(): lax.all_to_all(gathered, 'band', split_axis=1, concat_axis=2, tiled=True)  105 us
    all_gather x1, waiting for transfers between devices, local(): gathered = lax.all_gather(coefficients, 'walk', axis=1, tiled=True)  79.9 us
    dynamic_update_slice x16, local copies, waits for them, and re-layouts, local(): lax.map(lambda coords: orbital_block(coords[0], coords[1], lat_x, lat_y,...  60.7 us
    all_to_all x3, local copies, waits for them, and re-layouts, local(): lax.all_to_all(gathered, 'band', split_axis=1, concat_axis=2, tiled=True)  41.4 us
  transfers between devices with their start and end apart: 4, of which 4 were waited for; matrix products, arithmetic and copies ran while one was open for 0% of the time, Pallas kernels for 0%

commit v1 on v0

--- a/solution.py
+++ b/solution.py
@@ -64,7 +64,10 @@
     band_index = lax.axis_index("band")
     occ_flat = occupied.reshape(-1)
     wave_count = lattice.shape[1]
-    gathered = lax.all_gather(coefficients, "walk", axis=1, tiled=True)
+    devices = lax.axis_size("walk")
+    pieces = jnp.stack([coefficients for _ in range(devices)])
+    pieces = lax.all_to_all(pieces, "walk", split_axis=0, concat_axis=0)
+    gathered = jnp.concatenate(pieces, axis=1)
     band_panel = lax.all_to_all(gathered, "band", split_axis=1, concat_axis=2, tiled=True)
     picked = jnp.take(band_panel, occ_flat, axis=2)
     local_lattice = lax.dynamic_slice_in_dim(

time: 901 us -> 961 us (1.067)
  blocking collectives: 0 us -> 116 us
  waiting for transfers between devices: 433 us -> 353 us
  local copies, waits for them, and re-layouts: 127 us -> 151 us
    all_to_all x0 -> x1, blocking collectives: none -> 116 us  [local(): pieces = lax.all_to_all(pieces, 'walk', split_axis=0, concat_axis=0)]
    all_gather x1 -> x0, waiting for transfers between devices: 79.9 us -> none  [local(): gathered = lax.all_gather(coefficients, 'walk', axis=1, tiled=True)]
    reshape x0 -> x1, local copies, waits for them, and re-layouts: none -> 18.2 us  [local(): gathered = jnp.concatenate(pieces, axis=1)]
  transfers between devices with their start and end apart: 4 -> 3, of which waited for: 4 -> 3; matrix products, arithmetic and copies ran while one was open for 0% -> 0% of each run, Pallas kernels for 0% -> 0%
where the time goes in v1:
time: 961 us; the launch traced here: 951 us
  waiting for transfers between devices  353 us (37%)
  matrix products  282 us (29%)
  local copies, waits for them, and re-layouts  151 us (16%)
  blocking collectives  116 us (12%)
  loops' own time  25.6 us (3%)
  between operations  13.7 us (1%)
    dot_general x8, matrix products, orbital_block(): jnp.dot(sine_part, right_sin, precision=lax.Precision.HIGHEST, preferred_...  147 us
    psum x1, waiting for transfers between devices, local(): return lax.psum(gradient, 'walk')  134 us
    dot_general x8, matrix products, orbital_block(): jnp.dot(cosine, right_cos, precision=lax.Precision.HIGHEST, preferred_ele...  131 us
    all_to_all x1, blocking collectives, local(): pieces = lax.all_to_all(pieces, 'walk', split_axis=0, concat_axis=0)  116 us
    psum x1, waiting for transfers between devices, local(): orbitals = lax.psum(partial_value, 'band')  115 us
    all_to_all x1, waiting for transfers between devices, local(): lax.all_to_all(gathered, 'band', split_axis=1, concat_axis=2, tiled=True)  104 us
    dynamic_update_slice x16, local copies, waits for them, and re-layouts, local(): lax.map(lambda coords: orbital_block(coords[0], coords[1], lat_x, lat_y,...  60.7 us
    all_to_all x3, local copies, waits for them, and re-layouts, local(): lax.all_to_all(gathered, 'band', split_axis=1, concat_axis=2, tiled=True)  41.1 us
  transfers between devices with their start and end apart: 3, of which 3 were waited for; matrix products, arithmetic and copies ran while one was open for 0% of the time, Pallas kernels for 0%

profile of v1, /device:TPU:0, one launch (start us, length us, event | category | flops | bytes accessed | tf_op | source)
XLA Modules:
  0.0 951.2 jit_solution(10290788740964632432)
XLA Ops:
  9.8 115.9 %all_to_all.23 = bf16[16,2,1152,128]{3,2,1,0:T(8,128)(2,1)} all-to-all(bf16[16,2,1152,128]{3,2,1,0:T(8,128)(2,1)S(1)} %stack.2), channel_id=1, replica_groups=mesh['walk'=16,'band'=8] {'walk'}, dimensions={0} | all-to-all | bytes 18874368 | tf_op jit(solution)/shard_map/all_to_all | solution.py:69
  125.7 8.3 copy.31
  134.1 18.2 %copy.32 = bf16[2,18432,128]{2,0,1:T(2,128)(2,1)} copy(bf16[2,18432,128]{2,1,0:T(8,128)(2,1)} %bitcast.36) | data formatting | bytes 18874368 | tf_op jit(solution)/shard_map/reshape | solution.py:70
  158.7 104.0 %all-to-all-done.1 = bf16[2,18432,128]{2,0,1:T(2,128)(2,1)} async-done(((bf16[2,18432,128]{2,0,1:T(2,128)(2,1)}), bf16[2,18432,128]{2,0,1:T(2,128)(2,1)}, u32[]{:S(2)}, u32[]{:S(2)}) %all-to-all-start.1) | async-done | bytes 9437216 | tf_op jit(solution)/shard_map/all_to_all | solution.py:71
  262.8 10.1 %copy.33 = bf16[2,18432,128]{2,1,0:T(8,128)(2,1)} copy(bf16[2,18432,128]{2,0,1:T(2,128)(2,1)} %all-to-all-done.1) | data formatting | bytes 18874368 | tf_op jit(solution)/shard_map/all_to_all | solution.py:71
  272.9 12.6 %copy.34 = bf16[2,2304,8,128]{1,3,2,0:T(8,128)(2,1)} copy(bf16[2,2304,8,128]{3,1,2,0:T(8,128)(2,1)} %bitcast.37) | data formatting | bytes 18874368 | tf_op jit(solution)/shard_map/all_to_all | solution.py:71
  285.5 18.4 %copy.35 = bf16[2,2304,1024]{1,0,2:T(2,128)(2,1)} copy(bf16[2,2304,1024]{1,2,0:T(8,128)(2,1)} %bitcast.38) | data formatting | bytes 18874368 | tf_op jit(solution)/shard_map/all_to_all | solution.py:71
  318.5 364.3 %while.10 = (s32[]{:T(128)}, f32[8,384,192]{1,0,2:T(8,128)}, f32[8,384]{1,0:T(8,128)S(1)}, f32[2304]{0:T(1024)S(1)}, f32[8,384]{1,0:T(8,128)S(1)}, /*index=5*/f3...) while((s32[]{:T(128)}, f32[8,384,192]{1,0,2:T(8,128)}, ...), condition=%wide.region_1.2_spmd, body=%wide.region_0.1_spmd.sunk | while | flops 4084015104 | bytes 12730505 | solution.py:85
  341.2 18.3 %fusion.54 = f32[384,192]{0,1:T(8,128)S(1)} fusion(f32[2304,192]{1,0:T(8,128)} %get-tuple-element.200, f32[2304]{0:T(1024)S(1)} %get-tuple-element.198, f32[384]{0:T(512)S(1)} %get-tuple-element.171, f32[2304]{0:T(1024)S(1)} %get-tuple-element.196, f32[384]{0:T(512)S(1)} %get-tuple-element.172), kind=kOutput, calls=%fused_computation.1.clone.1 | convolution fusion | flops 2041970688 | bytes 2085888 | tf_op jit(solution)/shard_map/while/body/eval_jaxpr/dot_general | solution.py:17
  359.5 16.4 %fusion.55 = f32[1,384,192]{1,2,0:T(8,128)S(1)} fusion(f32[384,192]{0,1:T(8,128)S(1)} %fusion.54, f32[2304,192]{1,0:T(8,128)S(1)} %copy-done.2, f32[2304]{0:T(1024)S(1)} %get-tuple-element.198, f32[384]{0:T(512)S(1)} %get-tuple-element.171, f32[2304]{0:T(1024)S(1)} %get-tuple-element.196, f32[384]{0:T(512)S(1)} %get-tuple-element.172), kind=kOutput, calls=%fused_computation.17.clone.1 | convolution fusion | flops 2042044416 | bytes 2380800 | tf_op jit(solution)/shard_map/while/body/eval_jaxpr/dot_general | solution.py:14
  376.2 7.3 dynamic_update_slice.5
  383.5 18.3 %fusion.54 = f32[384,192]{0,1:T(8,128)S(1)} fusion(f32[2304,192]{1,0:T(8,128)} %get-tuple-element.200, f32[2304]{0:T(1024)S(1)} %get-tuple-element.198, f32[384]{0:T(512)S(1)} %get-tuple-element.171, f32[2304]{0:T(1024)S(1)} %get-tuple-element.196, f32[384]{0:T(512)S(1)} %get-tuple-element.172), kind=kOutput, calls=%fused_computation.1.clone.1 | convolution fusion | flops 2041970688 | bytes 2085888 | tf_op jit(solution)/shard_map/while/body/eval_jaxpr/dot_general | solution.py:17
  401.9 16.4 %fusion.55 = f32[1,384,192]{1,2,0:T(8,128)S(1)} fusion(f32[384,192]{0,1:T(8,128)S(1)} %fusion.54, f32[2304,192]{1,0:T(8,128)S(1)} %copy-done.2, f32[2304]{0:T(1024)S(1)} %get-tuple-element.198, f32[384]{0:T(512)S(1)} %get-tuple-element.171, f32[2304]{0:T(1024)S(1)} %get-tuple-element.196, f32[384]{0:T(512)S(1)} %get-tuple-element.172), kind=kOutput, calls=%fused_computation.17.clone.1 | convolution fusion | flops 2042044416 | bytes 2380800 | tf_op jit(solution)/shard_map/while/body/eval_jaxpr/dot_general | solution.py:14
  418.6 7.3 dynamic_update_slice.5
  425.9 18.3 %fusion.54 = f32[384,192]{0,1:T(8,128)S(1)} fusion(f32[2304,192]{1,0:T(8,128)} %get-tuple-element.200, f32[2304]{0:T(1024)S(1)} %get-tuple-element.198, f32[384]{0:T(512)S(1)} %get-tuple-element.171, f32[2304]{0:T(1024)S(1)} %get-tuple-element.196, f32[384]{0:T(512)S(1)} %get-tuple-element.172), kind=kOutput, calls=%fused_computation.1.clone.1 | convolution fusion | flops 2041970688 | bytes 2085888 | tf_op jit(solution)/shard_map/while/body/eval_jaxpr/dot_general | solution.py:17
  444.3 16.4 %fusion.55 = f32[1,384,192]{1,2,0:T(8,128)S(1)} fusion(f32[384,192]{0,1:T(8,128)S(1)} %fusion.54, f32[2304,192]{1,0:T(8,128)S(1)} %copy-done.2, f32[2304]{0:T(1024)S(1)} %get-tuple-element.198, f32[384]{0:T(512)S(1)} %get-tuple-element.171, f32[2304]{0:T(1024)S(1)} %get-tuple-element.196, f32[384]{0:T(512)S(1)} %get-tuple-element.172), kind=kOutput, calls=%fused_computation.17.clone.1 | convolution fusion | flops 2042044416 | bytes 2380800 | tf_op jit(solution)/shard_map/while/body/eval_jaxpr/dot_general | solution.py:14
  468.3 18.3 %fusion.54 = f32[384,192]{0,1:T(8,128)S(1)} fusion(f32[2304,192]{1,0:T(8,128)} %get-tuple-element.200, f32[2304]{0:T(1024)S(1)} %get-tuple-element.198, f32[384]{0:T(512)S(1)} %get-tuple-element.171, f32[2304]{0:T(1024)S(1)} %get-tuple-element.196, f32[384]{0:T(512)S(1)} %get-tuple-element.172), kind=kOutput, calls=%fused_computation.1.clone.1 | convolution fusion | flops 2041970688 | bytes 2085888 | tf_op jit(solution)/shard_map/while/body/eval_jaxpr/dot_general | solution.py:17
  486.6 16.4 %fusion.55 = f32[1,384,192]{1,2,0:T(8,128)S(1)} fusion(f32[384,192]{0,1:T(8,128)S(1)} %fusion.54, f32[2304,192]{1,0:T(8,128)S(1)} %copy-done.2, f32[2304]{0:T(1024)S(1)} %get-tuple-element.198, f32[384]{0:T(512)S(1)} %get-tuple-element.171, f32[2304]{0:T(1024)S(1)} %get-tuple-element.196, f32[384]{0:T(512)S(1)} %get-tuple-element.172), kind=kOutput, calls=%fused_computation.17.clone.1 | convolution fusion | flops 2042044416 | bytes 2380800 | tf_op jit(solution)/shard_map/while/body/eval_jaxpr/dot_general | solution.py:14
  510.7 18.3 %fusion.54 = f32[384,192]{0,1:T(8,128)S(1)} fusion(f32[2304,192]{1,0:T(8,128)} %get-tuple-element.200, f32[2304]{0:T(1024)S(1)} %get-tuple-element.198, f32[384]{0:T(512)S(1)} %get-tuple-element.171, f32[2304]{0:T(1024)S(1)} %get-tuple-element.196, f32[384]{0:T(512)S(1)} %get-tuple-element.172), kind=kOutput, calls=%fused_computation.1.clone.1 | convolution fusion | flops 2041970688 | bytes 2085888 | tf_op jit(solution)/shard_map/while/body/eval_jaxpr/dot_general | solution.py:17
  529.0 16.4 %fusion.55 = f32[1,384,192]{1,2,0:T(8,128)S(1)} fusion(f32[384,192]{0,1:T(8,128)S(1)} %fusion.54, f32[2304,192]{1,0:T(8,128)S(1)} %copy-done.2, f32[2304]{0:T(1024)S(1)} %get-tuple-element.198, f32[384]{0:T(512)S(1)} %get-tuple-element.171, f32[2304]{0:T(1024)S(1)} %get-tuple-element.196, f32[384]{0:T(512)S(1)} %get-tuple-element.172), kind=kOutput, calls=%fused_computation.17.clone.1 | convolution fusion | flops 2042044416 | bytes 2380800 | tf_op jit(solution)/shard_map/while/body/eval_jaxpr/dot_general | solution.py:14
  545.7 7.3 dynamic_update_slice.5
  553.0 18.3 %fusion.54 = f32[384,192]{0,1:T(8,128)S(1)} fusion(f32[2304,192]{1,0:T(8,128)} %get-tuple-element.200, f32[2304]{0:T(1024)S(1)} %get-tuple-element.198, f32[384]{0:T(512)S(1)} %get-tuple-element.171, f32[2304]{0:T(1024)S(1)} %get-tuple-element.196, f32[384]{0:T(512)S(1)} %get-tuple-element.172), kind=kOutput, calls=%fused_computation.1.clone.1 | convolution fusion | flops 2041970688 | bytes 2085888 | tf_op jit(solution)/shard_map/while/body/eval_jaxpr/dot_general | solution.py:17
  571.4 16.4 %fusion.55 = f32[1,384,192]{1,2,0:T(8,128)S(1)} fusion(f32[384,192]{0,1:T(8,128)S(1)} %fusion.54, f32[2304,192]{1,0:T(8,128)S(1)} %copy-done.2, f32[2304]{0:T(1024)S(1)} %get-tuple-element.198, f32[384]{0:T(512)S(1)} %get-tuple-element.171, f32[2304]{0:T(1024)S(1)} %get-tuple-element.196, f32[384]{0:T(512)S(1)} %get-tuple-element.172), kind=kOutput, calls=%fused_computation.17.clone.1 | convolution fusion | flops 2042044416 | bytes 2380800 | tf_op jit(solution)/shard_map/while/body/eval_jaxpr/dot_general | solution.py:14
  588.1 7.3 dynamic_update_slice.5
  595.4 18.3 %fusion.54 = f32[384,192]{0,1:T(8,128)S(1)} fusion(f32[2304,192]{1,0:T(8,128)} %get-tuple-element.200, f32[2304]{0:T(1024)S(1)} %get-tuple-element.198, f32[384]{0:T(512)S(1)} %get-tuple-element.171, f32[2304]{0:T(1024)S(1)} %get-tuple-element.196, f32[384]{0:T(512)S(1)} %get-tuple-element.172), kind=kOutput, calls=%fused_computation.1.clone.1 | convolution fusion | flops 2041970688 | bytes 2085888 | tf_op jit(solution)/shard_map/while/body/eval_jaxpr/dot_general | solution.py:17
  613.8 16.4 %fusion.55 = f32[1,384,192]{1,2,0:T(8,128)S(1)} fusion(f32[384,192]{0,1:T(8,128)S(1)} %fusion.54, f32[2304,192]{1,0:T(8,128)S(1)} %copy-done.2, f32[2304]{0:T(1024)S(1)} %get-tuple-element.198, f32[384]{0:T(512)S(1)} %get-tuple-element.171, f32[2304]{0:T(1024)S(1)} %get-tuple-element.196, f32[384]{0:T(512)S(1)} %get-tuple-element.172), kind=kOutput, calls=%fused_computation.17.clone.1 | convolution fusion | flops 2042044416 | bytes 2380800 | tf_op jit(solution)/shard_map/while/body/eval_jaxpr/dot_general | solution.py:14
  630.5 7.3 dynamic_update_slice.5
  637.8 18.3 %fusion.54 = f32[384,192]{0,1:T(8,128)S(1)} fusion(f32[2304,192]{1,0:T(8,128)} %get-tuple-element.200, f32[2304]{0:T(1024)S(1)} %get-tuple-element.198, f32[384]{0:T(512)S(1)} %get-tuple-element.171, f32[2304]{0:T(1024)S(1)} %get-tuple-element.196, f32[384]{0:T(512)S(1)} %get-tuple-element.172), kind=kOutput, calls=%fused_computation.1.clone.1 | convolution fusion | flops 2041970688 | bytes 2085888 | tf_op jit(solution)/shard_map/while/body/eval_jaxpr/dot_general | solution.py:17
  656.1 16.4 %fusion.55 = f32[1,384,192]{1,2,0:T(8,128)S(1)} fusion(f32[384,192]{0,1:T(8,128)S(1)} %fusion.54, f32[2304,192]{1,0:T(8,128)S(1)} %copy-done.2, f32[2304]{0:T(1024)S(1)} %get-tuple-element.198, f32[384]{0:T(512)S(1)} %get-tuple-element.171, f32[2304]{0:T(1024)S(1)} %get-tuple-element.196, f32[384]{0:T(512)S(1)} %get-tuple-element.172), kind=kOutput, calls=%fused_computation.17.clone.1 | convolution fusion | flops 2042044416 | bytes 2380800 | tf_op jit(solution)/shard_map/while/body/eval_jaxpr/dot_general | solution.py:14
  672.9 7.3 dynamic_update_slice.5
  689.3 114.8 %all-reduce.3.cloned.1.call-done = f32[3072,192]{0,1:T(8,128)} async-done(((f32[3072,192]{0,1:T(8,128)}), f32[3072,192]{0,1:T(8,128)}) %all-reduce.3.cloned.1.call-update) | async-done | bytes 2359312 | tf_op jit(solution)/shard_map/psum | solution.py:91
  808.8 133.8 %all-reduce.5.cloned.1.call-done = f32[256,192]{0,1:T(8,128)} async-done(((f32[256,192]{0,1:T(8,128)}), f32[256,192]{0,1:T(8,128)}) %all-reduce.5.cloned.1.call-update) | async-done | bytes 196624 | tf_op jit(solution)/shard_map/psum | solution.py:93
  (77 shorter events, 54.3 us)
Async XLA Ops:
  6.5 680.5 %copy-start = (bf16[3072,256]{1,0:T(8,128)(2,1)S(1)}, bf16[3072,256]{1,0:T(8,128)(2,1)}, u32[]{:S(2)}) copy-start(bf16[3072,256]{1,0:T(8,128)(2,1)} %param.14) | copy-start | bytes 4718596
  152.3 5.3 copy-start.6
  152.3 5.4 copy-start.4
  152.3 110.5 %all-to-all-start.1 = ((bf16[2,18432,128]{2,0,1:T(2,128)(2,1)}), bf16[2,18432,128]{2,0,1:T(2,128)(2,1)}, u32[]{:S(2)}, u32[]{:S(2)}) async-start(bf16[2,18432,128]{2,0,1:T(2,128)(2,1)} %copy.32), calls=%async_computation.1 | async-start | bytes 18874368 | tf_op jit(solution)/shard_map/all_to_all | solution.py:71
  157.5 646.6 %all-reduce.3.cloned.1.call-start = ((), (), s32[]{:S(2)}) async-start(), calls=%async_computation.2 | async-start | bytes 4718592 | tf_op jit(solution)/shard_map/psum | solution.py:91
  341.2 18.3 %copy-start.2 = (f32[2304,192]{1,0:T(8,128)S(1)}, f32[2304,192]{1,0:T(8,128)}, u32[]{:S(2)}) copy-start(f32[2304,192]{1,0:T(8,128)} %get-tuple-element.199) | copy-start | bytes 5308420 | tf_op jit(solution)/shard_map/while
  383.5 18.3 %copy-start.2 = (f32[2304,192]{1,0:T(8,128)S(1)}, f32[2304,192]{1,0:T(8,128)}, u32[]{:S(2)}) copy-start(f32[2304,192]{1,0:T(8,128)} %get-tuple-element.199) | copy-start | bytes 5308420 | tf_op jit(solution)/shard_map/while
  425.9 18.3 %copy-start.2 = (f32[2304,192]{1,0:T(8,128)S(1)}, f32[2304,192]{1,0:T(8,128)}, u32[]{:S(2)}) copy-start(f32[2304,192]{1,0:T(8,128)} %get-tuple-element.199) | copy-start | bytes 5308420 | tf_op jit(solution)/shard_map/while
  468.3 18.3 %copy-start.2 = (f32[2304,192]{1,0:T(8,128)S(1)}, f32[2304,192]{1,0:T(8,128)}, u32[]{:S(2)}) copy-start(f32[2304,192]{1,0:T(8,128)} %get-tuple-element.199) | copy-start | bytes 5308420 | tf_op jit(solution)/shard_map/while
  510.7 18.3 %copy-start.2 = (f32[2304,192]{1,0:T(8,128)S(1)}, f32[2304,192]{1,0:T(8,128)}, u32[]{:S(2)}) copy-start(f32[2304,192]{1,0:T(8,128)} %get-tuple-element.199) | copy-start | bytes 5308420 | tf_op jit(solution)/shard_map/while
  553.0 18.3 %copy-start.2 = (f32[2304,192]{1,0:T(8,128)S(1)}, f32[2304,192]{1,0:T(8,128)}, u32[]{:S(2)}) copy-start(f32[2304,192]{1,0:T(8,128)} %get-tuple-element.199) | copy-start | bytes 5308420 | tf_op jit(solution)/shard_map/while
  595.4 18.3 %copy-start.2 = (f32[2304,192]{1,0:T(8,128)S(1)}, f32[2304,192]{1,0:T(8,128)}, u32[]{:S(2)}) copy-start(f32[2304,192]{1,0:T(8,128)} %get-tuple-element.199) | copy-start | bytes 5308420 | tf_op jit(solution)/shard_map/while
  637.8 18.3 %copy-start.2 = (f32[2304,192]{1,0:T(8,128)S(1)}, f32[2304,192]{1,0:T(8,128)}, u32[]{:S(2)}) copy-start(f32[2304,192]{1,0:T(8,128)} %get-tuple-element.199) | copy-start | bytes 5308420 | tf_op jit(solution)/shard_map/while
  686.3 0.7 copy-start.5
  686.3 0.9 copy-start.3
  686.3 256.3 %all-reduce.5.cloned.1.call-start = ((), (), s32[]{:S(2)}) async-start(), calls=%async_computation.3 | async-start | bytes 393216 | tf_op jit(solution)/shard_map/psum | solution.py:93
  804.1 2.4 copy-start.1
Sparse Core Ops, SparseCore 0:
  686.4 117.6 all-reduce.2
  808.9 133.5 all-reduce.4
